TPU v7x, 128 devices: a whole 4x4x4 slice. The times are simulated.
128 devices in a mesh: row: 16 (over z, y), col: 8 (over x, core).
Axes of the slice: x: 4, y: 4, z: 4, core: 2. Of those that a mesh axis runs over, the one named last changes fastest.
Arguments:
- hidden: bfloat16 [4096, 8192], P('row', 'col'), may hold values from -96 to 96
- norm_gain: bfloat16 [8192], P('col'), may hold values from 0.5 to 1.5
- w_query: bfloat16 [8192, 4096], P('row', 'col')
- w_key: bfloat16 [8192, 4096], P('row', 'col')
- w_value: bfloat16 [8192, 4096], P('row', 'col'), may hold values from -0.0625 to 0.0625
- w_out: bfloat16 [4096, 8192], P('row', 'col'), may hold values from -0.09375 to 0.09375
Outputs:
- context: bfloat16 [4096, 4096], P('row', 'col')
- layer_out: bfloat16 [4096, 8192], P('row', 'col')
All inputs are finite; a program needn't handle non-finite values.
Results may differ from a plain program's by a relative error of at most 0.04.
Values may be sent and summed in bfloat16 or wider, within the bound.
A program may use at most 128 MiB of HBM per device.

v0:
```python
import math
import jax
import jax.numpy as jnp
from jax import lax
from jax.sharding import PartitionSpec as P

HD = 128
norm_epsilon = 1e-05


def rows_first(arrays, axis, dims):
    turned = [jnp.moveaxis(a, dim, 0) for a, dim in zip(arrays, dims)]
    widths = [t[0].size for t in turned]
    both = jnp.concatenate([t.reshape(-1, w) for t, w in zip(turned, widths)], axis=1)
    result = lax.all_gather(both, axis, axis=0, tiled=True)
    parts = jnp.split(result, [sum(widths[:k]) for k in range(1, len(widths))], axis=1)
    return tuple(
        (
            jnp.moveaxis(b.reshape(-1, *t.shape[1:]), 0, dim)
            for b, t, dim in zip(parts, turned, dims)
        )
    )


def side_by_side(arrays, axis, dim, along):
    widths = [a.shape[along] for a in arrays]
    both = jnp.concatenate(arrays, axis=along)
    result = lax.all_gather(both, axis, axis=dim, tiled=True)
    return tuple(jnp.split(result, [sum(widths[:k]) for k in range(1, len(widths))], axis=along))


def laid_out(parts, dim):
    parts = jnp.moveaxis(parts, 0, dim)
    lengths = parts.shape
    return parts.reshape(*lengths[:dim], lengths[dim] * lengths[dim + 1], *lengths[dim + 2 :])


def from_everyone(shard, axis):
    size = lax.axis_size(axis)
    return lax.all_to_all(
        jnp.broadcast_to(shard[None], (size, *shard.shape)), axis, 0, 0, tiled=True
    )


def gather_directly(shard, axis, dim):
    return laid_out(from_everyone(shard, axis), dim)


def rotary(values, positions):
    half = values.shape[-1] // 2
    freqs = jnp.exp(
        -math.log(10000.0) * 2.0 * jnp.arange(half, dtype=jnp.float32) / values.shape[-1]
    )
    angles = positions.astype(jnp.float32)[:, None] * freqs[None, :]
    cosine = jnp.cos(angles)[:, None, :]
    sine = jnp.sin(angles)[:, None, :]
    first = values[..., :half]
    second = values[..., half:]
    return jnp.concatenate(
        (first * cosine - second * sine, second * cosine + first * sine), axis=-1
    )


def blocked_sum(left, piece, block):
    count = piece.shape[0] // block
    split_left = left.reshape(left.shape[0], count, block)
    split_right = piece.reshape(count, block, piece.shape[1])
    terms = jnp.einsum("tbk,bkf->btf", split_left, split_right, preferred_element_type=jnp.float32)
    rounded = lax.optimization_barrier(terms.astype(jnp.bfloat16))
    return jnp.sum(rounded.astype(jnp.float32), axis=0)


def attend(carry, keys, values, queries, query_positions, key_positions, scale):
    peak, total, weighted = carry
    scores = jnp.einsum("qhd,khd->hqk", queries, keys, preferred_element_type=jnp.float32) * scale
    allowed = key_positions[None, :] <= query_positions[:, None]
    scores = jnp.where(allowed[None, :, :], scores, -jnp.inf)
    new_peak = jnp.maximum(peak, jnp.max(scores, axis=2))
    probs = jnp.exp(scores - new_peak[:, :, None])
    total = jnp.sum(probs, axis=2)
    weighted = jnp.einsum(
        "hqk,khd->hqd", probs.astype(jnp.bfloat16), values, preferred_element_type=jnp.float32
    )
    return (new_peak, total, weighted)


def start_state(heads_here, count):
    return (
        jnp.full((heads_here, count), -1e30, jnp.float32),
        jnp.zeros((heads_here, count), jnp.float32),
        jnp.zeros((heads_here, count, HD), jnp.float32),
    )


def finish(carry, count, heads_here):
    peak, total, weighted = carry
    return (
        (weighted / total[:, :, None])
        .transpose(1, 0, 2)
        .reshape(count, heads_here * HD)
        .astype(jnp.bfloat16)
    )


def on_device(hidden, norm_gain, w_query, w_key, w_value, w_out):
    rows = hidden.shape[0]
    residual = hidden.astype(jnp.float32)
    whole, gains = rows_first((hidden, norm_gain), "col", (1, 0))
    wide_rows = whole.astype(jnp.float32)
    mean_square = jnp.mean(wide_rows * wide_rows, axis=1, keepdims=True)
    normed = (
        wide_rows * lax.rsqrt(mean_square + norm_epsilon) * gains.astype(jnp.float32)[None, :]
    ).astype(jnp.bfloat16)
    block = w_query.shape[0]
    pieces = side_by_side((w_query, w_key, w_value), "row", 0, 1)
    segment = normed
    proj_q, proj_k, proj_v = tuple((blocked_sum(segment, piece, block) for piece in pieces))
    heads_here = w_query.shape[1] // HD
    row_index = lax.axis_index("row")
    first_row = row_index * rows
    positions = first_row + jnp.arange(rows, dtype=jnp.int32)
    query = rotary(proj_q.reshape(rows, heads_here, HD), positions).astype(jnp.bfloat16)
    keys_here = (
        rotary(proj_k.reshape(rows, heads_here, HD), positions)
        .astype(jnp.bfloat16)
        .reshape(rows, heads_here * HD)
    )
    values_here = proj_v.astype(jnp.bfloat16)
    scale = 1.0 / math.sqrt(HD)
    initial = start_state(heads_here, rows)
    pieces = side_by_side((keys_here, values_here), "row", 0, 1)
    keys = pieces[0].reshape(-1, heads_here, HD)
    values = pieces[1].reshape(-1, heads_here, HD)
    key_positions = jnp.arange(keys.shape[0], dtype=jnp.int32)
    folded = attend(initial, keys, values, query, positions, key_positions, scale)
    context = finish(folded, rows, heads_here)
    gathered_context = gather_directly(context, "col", 1)
    out_block = w_out.shape[0]
    segment = gathered_context
    attended = blocked_sum(segment, lax.all_gather(w_out, "row", axis=0, tiled=True), out_block)
    layer_out = (residual + attended).astype(jnp.bfloat16)
    return (context, layer_out)


def solution(mesh):
    placed = (
        P("row", "col"),
        P("col"),
        P("row", "col"),
        P("row", "col"),
        P("row", "col"),
        P("row", "col"),
    )
    return jax.shard_map(
        on_device,
        mesh=mesh,
        in_specs=placed,
        out_specs=(P("row", "col"), P("row", "col")),
        check_vma=False,
    )
```

profile of v0, /device:TPU:1, one launch (start us, length us, event | category | flops | bytes accessed | tf_op | source)
XLA Modules:
  0.0 393.5 jit_solution(4112995521757961650)
XLA Ops:
  7.2 0.7 reshape.144
  7.9 1.9 pad_maximum_fusion.1
  9.8 2.6 pad_maximum_fusion
  12.6 1.2 multiply_cosine_fusion
  13.8 32.3 %all-gather.5.cloned.1.call-done = bf16[8192,257]{0,1:T(8,128)(2,1)} async-done(((bf16[1024,257]{0,1:T(8,128)(2,1)}), bf16[8192,257]{0,1:T(8,128)(2,1)}) %all-gather.5.cloned.1.call-update) | async-done | bytes 4210704 | tf_op jit(solution)/shard_map/all_gather | solution.py:15
  46.1 3.1 fusion.3
  49.2 0.9 slice_convert_fusion
  50.1 5.4 %fusion.5 = bf16[8192,256]{0,1:T(8,128)(2,1)} fusion(f32[8192]{0:T(1024)S(1)} %bitcast.60, f32[256]{0:T(256)S(1)} %add_rsqrt_fusion, bf16[8192,257]{0,1:T(8,128)(2,1)} %all-gather.5.cloned.1.call-done), kind=kLoop, calls=%fused_computation.10 | loop fusion | flops 8388608 | bytes 8422400 | tf_op jit(solution)/shard_map/convert_element_type | solution.py:113
  55.6 146.4 %all-gather.7.cloned.1.call-done = bf16[8192,1536]{1,0:T(8,128)(2,1)} async-done(((bf16[512,1536]{1,0:T(8,128)(2,1)}), bf16[8192,1536]{1,0:T(8,128)(2,1)}) %all-gather.7.cloned.1.call-update) | async-done | bytes 25165840 | tf_op jit(solution)/shard_map/all_gather | solution.py:28
  201.9 12.4 %fusion.44 = (bf16[8192,512]{1,0:T(8,128)(2,1)S(1)}, bf16[8192,512]{1,0:T(8,128)(2,1)S(1)}, bf16[8192,512]{1,0:T(8,128)(2,1)}) fusion(bf16[8192,1536]{1,0:T(8,128)(2,1)} %all-gather.7.cloned.1.call-done), kind=kLoop, calls=%fused_computation.56 | loop fusion | bytes 50331648 | tf_op jit(solution)/shard_map/split | solution.py:29
  214.3 4.3 %fusion.24 = bf16[16,256,512]{2,1,0:T(8,128)(2,1)} fusion(bf16[16,512,512]{2,1,0:T(8,128)(2,1)S(1)} %bitcast.49, bf16[32,16,8,512]{3,2,1,0:T(8,128)(2,1)S(1)} %bitcast.51), kind=kOutput, calls=%fused_computation.28 | convolution fusion | flops 2149580800 | bytes 16777216 | tf_op jit(solution)/shard_map/tbk,bkf->btf/dot_general | solution.py:68
  218.6 2.3 fusion.18
  221.0 0.6 convert_reduce_fusion.2
  222.2 7.0 %fusion.21 = bf16[16,256,512]{2,1,0:T(8,128)(2,1)S(1)} fusion(bf16[16,512,512]{2,1,0:T(8,128)(2,1)} %bitcast.47, bf16[32,16,8,512]{3,2,1,0:T(8,128)(2,1)} %bitcast.50), kind=kOutput, calls=%fused_computation.27 | convolution fusion | flops 2149580800 | bytes 16777216 | tf_op jit(solution)/shard_map/tbk,bkf->btf/dot_general | solution.py:68
  229.2 0.6 convert_reduce_fusion.1
  231.2 2.8 reduce_sum.60
  234.1 0.9 pad_maximum_fusion.2
  235.6 0.7 iota_compare_fusion
  236.2 69.4 %all-gather.9.cloned.1.call-done = bf16[4096,1024]{1,0:T(8,128)(2,1)} async-done(((bf16[256,1024]{1,0:T(8,128)(2,1)}), bf16[4096,1024]{1,0:T(8,128)(2,1)}) %all-gather.9.cloned.1.call-update) | async-done | bytes 8388624 | tf_op jit(solution)/shard_map/all_gather | solution.py:28
  305.6 5.7 %fusion.45 = (bf16[4096,512]{1,0:T(8,128)(2,1)}, bf16[4096,512]{1,0:T(8,128)(2,1)}) fusion(bf16[4096,1024]{1,0:T(8,128)(2,1)} %all-gather.9.cloned.1.call-done), kind=kLoop, calls=%fused_computation.57 | loop fusion | bytes 16777216 | tf_op jit(solution)/shard_map/split | solution.py:29
  311.4 6.4 %copy.37 = bf16[4096,512]{0,1:T(8,128)(2,1)} copy(bf16[4096,512]{1,0:T(8,128)(2,1)} %get-tuple-element.12) | data formatting | bytes 8388608 | tf_op jit(solution)/shard_map/split | solution.py:29
  317.8 6.4 %copy.35 = bf16[4096,512]{0,1:T(8,128)(2,1)} copy(bf16[4096,512]{1,0:T(8,128)(2,1)} %get-tuple-element.11) | data formatting | bytes 8388608 | tf_op jit(solution)/shard_map/split | solution.py:29
  324.2 5.8 %fusion = (f32[4,256]{1,0:T(4,128)S(1)}, f32[4,256,4096]{2,1,0:T(8,128)S(1)}) fusion(pred[256,4096]{1,0:T(8,128)(4,1)S(1)} %iota_compare_fusion, bf16[4096,4,128]{0,2,1:T(8,128)(2,1)} %bitcast.44, bf16[256,4,64]{2,0,1:T(8,128)(2,1)S(1)} %get-tuple-element.14, bf16[256,4,64]{2,0,1:T(8,128)(2,1)S(1)} %get-tuple-element.13), kind=kOutput, calls=%fused_computation.3 | convolution fusion | flops 1086848000 | bytes 22286336 | tf_op jit(solution)/shard_map/qhd,khd->hqk/dot_general | solution.py:75
  330.0 4.4 %fusion.1 = f32[4,256]{1,0:T(4,128)S(1)} fusion(f32[4,256,4096]{2,1,0:T(8,128)S(1)} %get-tuple-element.26, f32[4,256]{1,0:T(4,128)S(1)} %broadcast_maximum_fusion, pred[256,4096]{1,0:T(8,128)(4,1)S(1)} %iota_compare_fusion), kind=kLoop, calls=%fused_computation.4 | loop fusion | flops 16776192 | bytes 17833984 | tf_op jit(solution)/shard_map/reduce_sum | solution.py:80
  334.5 6.7 %fusion.33 = bf16[256,4,128]{0,2,1:T(8,128)(2,1)S(1)} fusion(bf16[4096,4,128]{0,2,1:T(8,128)(2,1)} %bitcast.53, f32[4,256,4096]{2,1,0:T(8,128)S(1)} %get-tuple-element.26, f32[4,256]{1,0:T(4,128)S(1)} %broadcast_maximum_fusion, pred[256,4096]{1,0:T(8,128)(4,1)S(1)} %iota_compare_fusion, f32[256,4]{0,1:T(4,128)S(1)} %bitcast.61), kind=kOutput, calls=%fused_computation.33 | convolution fusion | flops 1090781184 | bytes 22290432 | tf_op jit(solution)/shard_map/hqk,khd->hqd/dot_general | solution.py:81
  341.1 1.5 broadcast_in_dim.15
  342.6 5.2 %all-to-all-start = ((bf16[8,256,512]{1,2,0:T(8,128)(2,1)}), bf16[8,256,512]{1,2,0:T(8,128)(2,1)S(1)}, u32[]{:S(2)}, u32[]{:S(2)}) async-start(bf16[8,256,512]{1,2,0:T(8,128)(2,1)} %broadcast_in_dim.15), calls=%async_computation | async-start | bytes 4194304 | tf_op jit(solution)/shard_map/all_to_all | solution.py:40
  347.8 0.8 copy.39
  348.7 29.5 %all-gather.11.cloned.1.call-done = bf16[4096,1024]{1,0:T(8,128)(2,1)} async-done(((bf16[256,1024]{1,0:T(8,128)(2,1)}), bf16[4096,1024]{1,0:T(8,128)(2,1)}) %all-gather.11.cloned.1.call-update) | async-done | bytes 8388624 | tf_op jit(solution)/shard_map/all_gather | solution.py:140
  378.2 5.8 %convolution_convert_fusion = bf16[16,256,1024]{2,1,0:T(8,128)(2,1)S(1)} fusion(bf16[256,16,256]{0,2,1:T(8,128)(2,1)S(1)} %bitcast.45, bf16[16,256,1024]{2,1,0:T(8,128)(2,1)} %bitcast.46), kind=kOutput, calls=%fused_computation.15 | convolution fusion | flops 2151677952 | bytes 18874368 | tf_op jit(solution)/shard_map/tbk,bkf->btf/dot_general | solution.py:68
  384.0 2.0 convert_reduce_fusion
  386.0 0.9 add_convert_fusion
  (33 shorter events, 2.8 us)
Async XLA Ops:
  7.2 38.9 %all-gather.5.cloned.1.call-start = ((), (), s32[]{:S(2)}) async-start(), calls=%async_computation.1 | async-start | bytes 4866048 | tf_op jit(solution)/shard_map/all_gather | solution.py:15
  9.8 192.1 %all-gather.7.cloned.1.call-start = ((), (), s32[]{:S(2)}) async-start(), calls=%async_computation.2 | async-start | bytes 26738688 | tf_op jit(solution)/shard_map/all_gather | solution.py:28
  12.5 293.2 %all-gather.9.cloned.1.call-start = ((), (), s32[]{:S(2)}) async-start(), calls=%async_computation.3 | async-start | bytes 8912896 | tf_op jit(solution)/shard_map/all_gather | solution.py:28
  201.9 12.4 %copy-start = (bf16[8192,256]{0,1:T(8,128)(2,1)S(1)}, bf16[8192,256]{0,1:T(8,128)(2,1)}, u32[]{:S(2)}) copy-start(bf16[8192,256]{0,1:T(8,128)(2,1)} %fusion.5) | copy-start | bytes 12582916
  229.2 1.3 copy-start.2
  229.2 1.3 copy-start.3
  235.0 143.2 %all-gather.11.cloned.1.call-start = ((), (), s32[]{:S(2)}) async-start(), calls=%async_computation.4 | async-start | bytes 8912896 | tf_op jit(solution)/shard_map/all_gather | solution.py:140
  342.6 35.5 %all-to-all-start = ((bf16[8,256,512]{1,2,0:T(8,128)(2,1)}), bf16[8,256,512]{1,2,0:T(8,128)(2,1)S(1)}, u32[]{:S(2)}, u32[]{:S(2)}) async-start(bf16[8,256,512]{1,2,0:T(8,128)(2,1)} %broadcast_in_dim.15), calls=%async_computation | async-start | bytes 4194304 | tf_op jit(solution)/shard_map/all_to_all | solution.py:40
  384.0 2.0 copy-start.1
Sparse Core Ops, SparseCore 0:
  9.9 36.1 all-gather.4
  48.2 153.6 all-gather.6
  235.1 70.5 all-gather.8
  307.6 70.5 all-gather.10
where the time goes:
time: 394 us; the launch traced here: 393 us
  waiting for transfers between devices  278 us (71%)
  local copies, waits for them, and re-layouts  35.5 us (9%)
  matrix products  31.9 us (8%)
  other arithmetic  28.6 us (7%)
  between operations  14 us (4%)
  starting transfers between devices  5.33 us (1%)
    all_gather x2, waiting for transfers between devices, side_by_side(): result = lax.all_gather(both, axis, axis=dim, tiled=True)  216 us
    all_gather x1, waiting for transfers between devices, rows_first(): result = lax.all_gather(both, axis, axis=0, tiled=True)  32.3 us
    split x4, local copies, waits for them, and re-layouts, side_by_side(): jnp.split(result, [sum(widths[:k]) for k in range(1, len(widths))], axis=...  31 us
    all_gather x1, waiting for transfers between devices, on_device(): lax.all_gather(w_out, 'row', axis=0, tiled=True)  29.5 us
    dot_general x4, matrix products, blocked_sum(): jnp.einsum('tbk,bkf->btf', split_left, split_right, preferred_element_typ...  19.4 us
  transfers between devices with their start and end apart: 5, of which 4 were waited for; matrix products, arithmetic and copies ran while one was open for 13% of the time, Pallas kernels for 0%

commit v1 on v0

--- a/solution.py
+++ b/solution.py
@@ -12,7 +12,9 @@
     turned = [jnp.moveaxis(a, dim, 0) for a, dim in zip(arrays, dims)]
     widths = [t[0].size for t in turned]
     both = jnp.concatenate([t.reshape(-1, w) for t, w in zip(turned, widths)], axis=1)
-    result = lax.all_gather(both, axis, axis=0, tiled=True)
+    result = jnp.concatenate(
+        lax.all_to_all(jnp.stack([both] * lax.axis_size(axis)), axis, 0, 0), axis=0
+    )
     parts = jnp.split(result, [sum(widths[:k]) for k in range(1, len(widths))], axis=1)
     return tuple(
         (

time: 394 us -> 372 us (0.944)
  waiting for transfers between devices: 278 us -> 230 us
  local copies, waits for them, and re-layouts: 35.5 us -> 48.9 us
  matrix products: 31.9 us -> 38.7 us
  starting transfers between devices: 5.33 us -> 11 us
    all_gather x2, waiting for transfers between devices: 216 us -> 150 us  [side_by_side(): result = lax.all_gather(both, axis, axis=dim, tiled=True)]
    all_to_all x0 -> x1, waiting for transfers between devices: none -> 49.7 us  [rows_first(): lax.all_to_all(jnp.stack([both] * lax.axis_size(axis)), axis, 0, 0)]
    all_gather x1 -> x0, waiting for transfers between devices: 32.3 us -> none  [rows_first(): result = lax.all_gather(both, axis, axis=0, tiled=True)]
    all_to_all x0 -> x1, local copies, waits for them, and re-layouts: none -> 7.88 us  [rows_first(): lax.all_to_all(jnp.stack([both] * lax.axis_size(axis)), axis, 0, 0)]
    dot_general x4, matrix products: 19.4 us -> 26.2 us  [blocked_sum(): jnp.einsum('tbk,bkf->btf', split_left, split_right, preferred_element_typ...]
    all_to_all x0 -> x1, starting transfers between devices: none -> 5.84 us  [rows_first(): lax.all_to_all(jnp.stack([both] * lax.axis_size(axis)), axis, 0, 0)]
  transfers between devices with their start and end apart: 5 -> 5, of which waited for: 4 -> 4; matrix products, arithmetic and copies ran while one was open for 13% -> 16% of each run, Pallas kernels for 0% -> 0%
where the time goes in v1:
time: 372 us; the launch traced here: 371 us
  waiting for transfers between devices  230 us (62%)
  local copies, waits for them, and re-layouts  48.9 us (13%)
  matrix products  38.7 us (10%)
  other arithmetic  28.2 us (8%)
  between operations  13.9 us (4%)
  starting transfers between devices  11 us (3%)
    all_gather x2, waiting for transfers between devices, side_by_side(): result = lax.all_gather(both, axis, axis=dim, tiled=True)  150 us
    all_to_all x1, waiting for transfers between devices, rows_first(): lax.all_to_all(jnp.stack([both] * lax.axis_size(axis)), axis, 0, 0)  49.7 us
    split x4, local copies, waits for them, and re-layouts, side_by_side(): jnp.split(result, [sum(widths[:k]) for k in range(1, len(widths))], axis=...  33.2 us
    all_gather x1, waiting for transfers between devices, on_device(): lax.all_gather(w_out, 'row', axis=0, tiled=True)  29.8 us
    dot_general x4, matrix products, blocked_sum(): jnp.einsum('tbk,bkf->btf', split_left, split_right, preferred_element_typ...  26.2 us
    reduce_sum x4, other arithmetic, blocked_sum(): return jnp.sum(rounded.astype(jnp.float32), axis=0)  8.26 us
    all_to_all x1, local copies, waits for them, and re-layouts, rows_first(): lax.all_to_all(jnp.stack([both] * lax.axis_size(axis)), axis, 0, 0)  7.88 us
  transfers between devices with their start and end apart: 5, of which 4 were waited for; matrix products, arithmetic and copies ran while one was open for 16% of the time, Pallas kernels for 0%

profile of v1, /device:TPU:1, one launch (start us, length us, event | category | flops | bytes accessed | tf_op | source)
XLA Modules:
  0.0 371.0 jit_solution(17740609961970122112)
XLA Ops:
  7.2 2.6 pad_maximum_fusion
  9.8 0.7 reshape.149
  10.5 1.1 pad_maximum_fusion.1
  11.6 2.6 stack.2
  14.2 5.8 %all-to-all-start = ((bf16[8,1024,257]{1,2,0:T(8,128)(2,1)}), bf16[8,1024,257]{1,2,0:T(8,128)(2,1)}, u32[]{:S(2)}, u32[]{:S(2)}) async-start(bf16[8,1024,257]{1,2,0:T(8,128)(2,1)} %stack.2), calls=%async_computation | async-start | bytes 8650752 | tf_op jit(solution)/shard_map/all_to_all | solution.py:16
  20.6 49.7 %all-to-all-done = bf16[8,1024,257]{1,2,0:T(8,128)(2,1)} async-done(((bf16[8,1024,257]{1,2,0:T(8,128)(2,1)}), bf16[8,1024,257]{1,2,0:T(8,128)(2,1)}, u32[]{:S(2)}, u32[]{:S(2)}) %all-to-all-start) | async-done | bytes 4210720 | tf_op jit(solution)/shard_map/all_to_all | solution.py:16
  70.2 7.9 %copy.23 = bf16[8,1024,257]{2,1,0:T(8,128)(2,1)} copy(bf16[8,1024,257]{1,2,0:T(8,128)(2,1)} %all-to-all-done) | data formatting | bytes 8421376 | tf_op jit(solution)/shard_map/all_to_all | solution.py:16
  78.1 3.5 fusion.3
  81.6 2.2 convert_reduce_fusion.3
  83.9 2.6 fusion.5
  86.5 80.9 %all-gather.4.cloned.1.call-done = bf16[8192,1536]{1,0:T(8,128)(2,1)} async-done(((bf16[512,1536]{1,0:T(8,128)(2,1)}), bf16[8192,1536]{1,0:T(8,128)(2,1)}) %all-gather.4.cloned.1.call-update) | async-done | bytes 25165840 | tf_op jit(solution)/shard_map/all_gather | solution.py:30
  167.4 14.7 %fusion.26 = (bf16[8192,512]{1,0:T(8,128)(2,1)S(1)}, bf16[8192,512]{1,0:T(8,128)(2,1)}, bf16[8192,512]{1,0:T(8,128)(2,1)}) fusion(bf16[8192,1536]{1,0:T(8,128)(2,1)} %all-gather.4.cloned.1.call-done), kind=kLoop, calls=%fused_computation.47 | loop fusion | bytes 50331648 | tf_op jit(solution)/shard_map/split | solution.py:31
  182.7 4.3 %convolution_convert_fusion.3 = bf16[16,256,512]{2,1,0:T(8,128)(2,1)} fusion(bf16[256,16,512]{0,2,1:T(8,128)(2,1)S(1)} %bitcast.37, bf16[16,512,512]{2,1,0:T(8,128)(2,1)S(1)} %bitcast.43), kind=kOutput, calls=%fused_computation.20 | convolution fusion | flops 2149580800 | bytes 16777216 | tf_op jit(solution)/shard_map/tbk,bkf->btf/dot_general | solution.py:70
  187.0 2.8 convert_reduce_fusion.2
  190.5 7.0 %convolution_convert_fusion.2 = bf16[16,256,512]{2,1,0:T(8,128)(2,1)S(1)} fusion(bf16[256,16,512]{0,2,1:T(8,128)(2,1)} %bitcast.35, bf16[16,512,512]{2,1,0:T(8,128)(2,1)} %bitcast.42), kind=kOutput, calls=%fused_computation.19 | convolution fusion | flops 2149580800 | bytes 16777216 | tf_op jit(solution)/shard_map/tbk,bkf->btf/dot_general | solution.py:70
  199.5 9.1 %convolution_convert_fusion.1 = bf16[16,256,512]{2,1,0:T(8,128)(2,1)} fusion(bf16[256,16,512]{0,2,1:T(8,128)(2,1)} %bitcast.36, bf16[16,512,512]{2,1,0:T(8,128)(2,1)} %bitcast.41), kind=kOutput, calls=%fused_computation.18 | convolution fusion | flops 2149580800 | bytes 16777216 | tf_op jit(solution)/shard_map/tbk,bkf->btf/dot_general | solution.py:70
  208.6 2.8 reduce_sum.60
  211.5 0.9 pad_maximum_fusion.2
  213.8 69.3 %all-gather.6.cloned.1.call-done = bf16[4096,1024]{1,0:T(8,128)(2,1)} async-done(((bf16[256,1024]{1,0:T(8,128)(2,1)}), bf16[4096,1024]{1,0:T(8,128)(2,1)}) %all-gather.6.cloned.1.call-update) | async-done | bytes 8388624 | tf_op jit(solution)/shard_map/all_gather | solution.py:30
  283.0 5.7 %fusion.27 = (bf16[4096,512]{1,0:T(8,128)(2,1)}, bf16[4096,512]{1,0:T(8,128)(2,1)}) fusion(bf16[4096,1024]{1,0:T(8,128)(2,1)} %all-gather.6.cloned.1.call-done), kind=kLoop, calls=%fused_computation.48 | loop fusion | bytes 16777216 | tf_op jit(solution)/shard_map/split | solution.py:31
  288.7 6.4 %copy.35 = bf16[4096,512]{0,1:T(8,128)(2,1)} copy(bf16[4096,512]{1,0:T(8,128)(2,1)} %get-tuple-element.11) | data formatting | bytes 8388608 | tf_op jit(solution)/shard_map/split | solution.py:31
  295.2 6.4 %copy.37 = bf16[4096,512]{0,1:T(8,128)(2,1)} copy(bf16[4096,512]{1,0:T(8,128)(2,1)} %get-tuple-element.12) | data formatting | bytes 8388608 | tf_op jit(solution)/shard_map/split | solution.py:31
  301.6 5.8 %fusion = (f32[4,256]{1,0:T(4,128)S(1)}, f32[4,256,4096]{2,1,0:T(8,128)S(1)}) fusion(pred[256,4096]{1,0:T(8,128)(4,1)S(1)} %iota_compare_fusion, bf16[4096,4,128]{0,2,1:T(8,128)(2,1)} %bitcast.44, bf16[256,4,64]{2,0,1:T(8,128)(2,1)S(1)} %get-tuple-element.14, bf16[256,4,64]{2,0,1:T(8,128)(2,1)S(1)} %get-tuple-element.13), kind=kOutput, calls=%fused_computation.3 | convolution fusion | flops 1086848000 | bytes 22286336 | tf_op jit(solution)/shard_map/qhd,khd->hqk/dot_general | solution.py:77
  307.4 4.4 %fusion.1 = f32[4,256]{1,0:T(4,128)S(1)} fusion(f32[4,256,4096]{2,1,0:T(8,128)S(1)} %get-tuple-element.26, f32[4,256]{1,0:T(4,128)S(1)} %broadcast_maximum_fusion, pred[256,4096]{1,0:T(8,128)(4,1)S(1)} %iota_compare_fusion), kind=kLoop, calls=%fused_computation.4 | loop fusion | flops 16776192 | bytes 17833984 | tf_op jit(solution)/shard_map/reduce_sum | solution.py:82
  311.8 6.7 %fusion.15 = bf16[256,4,128]{0,2,1:T(8,128)(2,1)S(1)} fusion(bf16[4096,4,128]{0,2,1:T(8,128)(2,1)} %bitcast.47, f32[4,256,4096]{2,1,0:T(8,128)S(1)} %get-tuple-element.26, f32[4,256]{1,0:T(4,128)S(1)} %broadcast_maximum_fusion, pred[256,4096]{1,0:T(8,128)(4,1)S(1)} %iota_compare_fusion, f32[256,4]{0,1:T(4,128)S(1)} %bitcast.54), kind=kOutput, calls=%fused_computation.25 | convolution fusion | flops 1090781184 | bytes 22290432 | tf_op jit(solution)/shard_map/hqk,khd->hqd/dot_general | solution.py:83
  318.5 1.5 broadcast_in_dim.15
  320.0 5.1 %all-to-all-start.1 = ((bf16[8,256,512]{1,2,0:T(8,128)(2,1)}), bf16[8,256,512]{1,2,0:T(8,128)(2,1)S(1)}, u32[]{:S(2)}, u32[]{:S(2)}) async-start(bf16[8,256,512]{1,2,0:T(8,128)(2,1)} %broadcast_in_dim.15), calls=%async_computation.1 | async-start | bytes 4194304 | tf_op jit(solution)/shard_map/all_to_all | solution.py:42
  325.1 0.8 copy.39
  326.0 29.8 %all-gather.8.cloned.1.call-done = bf16[4096,1024]{1,0:T(8,128)(2,1)} async-done(((bf16[256,1024]{1,0:T(8,128)(2,1)}), bf16[4096,1024]{1,0:T(8,128)(2,1)}) %all-gather.8.cloned.1.call-update) | async-done | bytes 8388624 | tf_op jit(solution)/shard_map/all_gather | solution.py:142
  355.7 5.8 %convolution_convert_fusion = bf16[16,256,1024]{2,1,0:T(8,128)(2,1)S(1)} fusion(bf16[256,16,256]{0,2,1:T(8,128)(2,1)S(1)} %bitcast.45, bf16[16,256,1024]{2,1,0:T(8,128)(2,1)} %bitcast.46), kind=kOutput, calls=%fused_computation.15 | convolution fusion | flops 2151677952 | bytes 18874368 | tf_op jit(solution)/shard_map/tbk,bkf->btf/dot_general | solution.py:70
  361.5 2.0 convert_reduce_fusion
  363.5 0.9 add_convert_fusion
  (32 shorter events, 5.2 us)
Async XLA Ops:
  7.2 160.2 %all-gather.4.cloned.1.call-start = ((), (), s32[]{:S(2)}) async-start(), calls=%async_computation.2 | async-start | bytes 26738688 | tf_op jit(solution)/shard_map/all_gather | solution.py:30
  14.2 56.1 %all-to-all-start = ((bf16[8,1024,257]{1,2,0:T(8,128)(2,1)}), bf16[8,1024,257]{1,2,0:T(8,128)(2,1)}, u32[]{:S(2)}, u32[]{:S(2)}) async-start(bf16[8,1024,257]{1,2,0:T(8,128)(2,1)} %stack.2), calls=%async_computation | async-start | bytes 8650752 | tf_op jit(solution)/shard_map/all_to_all | solution.py:16
  20.0 263.0 %all-gather.6.cloned.1.call-start = ((), (), s32[]{:S(2)}) async-start(), calls=%async_computation.3 | async-start | bytes 8912896 | tf_op jit(solution)/shard_map/all_gather | solution.py:30
  78.1 5.8 %copy-start.1 = (bf16[8,1024,257]{2,1,0:T(8,128)(2,1)S(1)}, bf16[8,1024,257]{2,1,0:T(8,128)(2,1)}, u32[]{:S(2)}) copy-start(bf16[8,1024,257]{2,1,0:T(8,128)(2,1)} %copy.23) | copy-start | bytes 12632068
  167.4 15.3 %copy-start = (bf16[8192,256]{1,0:T(8,128)(2,1)S(1)}, bf16[8192,256]{1,0:T(8,128)(2,1)}, u32[]{:S(2)}) copy-start(bf16[8192,256]{1,0:T(8,128)(2,1)} %fusion.5) | copy-start | bytes 12582916
  212.4 143.4 %all-gather.8.cloned.1.call-start = ((), (), s32[]{:S(2)}) async-start(), calls=%async_computation.4 | async-start | bytes 8912896 | tf_op jit(solution)/shard_map/all_gather | solution.py:142
  320.0 35.7 %all-to-all-start.1 = ((bf16[8,256,512]{1,2,0:T(8,128)(2,1)}), bf16[8,256,512]{1,2,0:T(8,128)(2,1)S(1)}, u32[]{:S(2)}, u32[]{:S(2)}) async-start(bf16[8,256,512]{1,2,0:T(8,128)(2,1)} %broadcast_in_dim.15), calls=%async_computation.1 | async-start | bytes 4194304 | tf_op jit(solution)/shard_map/all_to_all | solution.py:42
  361.5 2.0 copy-start.2
Sparse Core Ops, SparseCore 0:
  10.1 157.2 all-gather.3
  212.5 70.5 all-gather.5
  285.2 70.5 all-gather.7
